TPU v7x, 32 devices: a whole 2x2x4 slice. The times are simulated.
32 devices in a mesh: tok: 4 (over y, x), col: 8 (over z, core).
Axes of the slice: x: 2, y: 2, z: 4, core: 2. Of those that a mesh axis runs over, the one named last changes fastest.
Arguments:
- activations: bfloat16 [8192, 8192], P('tok', 'col'), may hold values from -60 to 60, as said below
- weight: bfloat16 [8192, 8192], P('tok', 'col'), may hold values from -6 to 6
- keep_mask: int32 [8192, 8192], P('tok', 'col'), may hold values from 0 to 1
Outputs:
- new_weight: bfloat16 [8192, 8192], P('tok', 'col')
Inputs may be any that keep to these rules, and one draw needn't show every extreme that they name: activations of calibration tokens.
All inputs are finite; a program needn't handle non-finite values.
Results may differ from a plain program's by a relative error of at most 0.00115.
Values may be sent and summed in bfloat16 or wider, within the bound.
No kernel may reach another device: no remote copies, remote signals or barrier semaphores. Data moves between devices by JAX's collectives and lax.ppermute only.
A program may use at most 128 MiB of HBM per device.

v0:
```python
import jax
import jax.numpy as jnp
from jax import lax
from jax.sharding import PartitionSpec as P

B = 1024
ITERS = 4


def per_device(activations, weight, keep_mask):
    highest = lax.Precision.HIGHEST
    n_col = lax.axis_size("col")
    n_tok = lax.axis_size("tok")
    tok_rows = activations.shape[0]
    panel_width = B // n_col
    total_count = tok_rows * n_tok
    partial_panel = lax.dot_general(
        activations,
        lax.all_gather(activations[:, :panel_width], "col", axis=1, tiled=True),
        (((0,), (0,)), ((), ())),
        preferred_element_type=jnp.float32,
    )
    block_part = lax.psum(partial_panel[:panel_width], "tok") / total_count
    diagonal_block = lax.all_gather(block_part, "col", axis=0, tiled=True)
    identity = jnp.eye(B, dtype=jnp.float32)
    damping = 0.01 * jnp.mean(jnp.diagonal(diagonal_block))
    damped = diagonal_block + damping * identity
    frobenius = jnp.sqrt(jnp.sum(damped * damped))
    col_index = lax.axis_index("col")
    row_ids = col_index * panel_width + lax.iota(jnp.int32, panel_width)
    iterate = (row_ids[:, None] == lax.iota(jnp.int32, B)[None, :]).astype(jnp.float32) / frobenius
    for sweep in range(ITERS):
        if sweep == 0:
            whole = identity / frobenius
        else:
            whole = lax.all_gather(iterate.astype(jnp.bfloat16), "col", axis=0, tiled=True).astype(
                iterate.dtype
            )
        product = jnp.dot(iterate, damped, precision=highest)
        iterate = 2.0 * iterate - jnp.dot(product, whole, precision=highest)
    inverse = lax.all_gather(iterate, "col", axis=0, tiled=True)
    remainder = lax.psum(partial_panel[panel_width:], "tok") / total_count
    hessian_panel = jnp.concatenate([block_part, remainder], axis=0)
    pruned = jnp.where(
        keep_mask[:, :panel_width] == 0, weight[:, :panel_width], jnp.zeros((), jnp.bfloat16)
    )
    pruned_panel = lax.all_gather(pruned, "col", axis=1, tiled=True).astype(jnp.float32)
    factor_rows = jnp.dot(pruned_panel, inverse, precision=highest)
    correction = lax.dot_general(
        factor_rows, hessian_panel, (((1,), (1,)), ((), ())), precision=highest
    )
    kept = keep_mask.astype(jnp.float32)
    return (kept * (weight.astype(jnp.float32) - correction)).astype(jnp.bfloat16)


def solution(mesh):
    return jax.shard_map(
        per_device,
        mesh=mesh,
        in_specs=(P("tok", "col"), P("tok", "col"), P("tok", "col")),
        out_specs=P("tok", "col"),
        check_vma=False,
    )
```

profile of v0, /device:TPU:0, one launch (start us, length us, event | category | flops | bytes accessed | tf_op | source)
XLA Modules:
  0.0 493.3 jit_solution(1033233946870937970)
XLA Ops:
  6.5 1.9 slice.17
  8.5 51.0 %all-gather.10.cloned.1.call-done = bf16[2048,1024]{1,0:T(8,128)(2,1)} async-done(((bf16[2048,128]{1,0:T(8,128)(2,1)}), bf16[2048,1024]{1,0:T(8,128)(2,1)}) %all-gather.10.cloned.1.call-update) | async-done | bytes 4194320 | tf_op jit(solution)/shard_map/all_gather | solution.py:19
  59.5 7.6 %fusion.31 = f32[1024,1024]{1,0:T(8,128)S(1)} fusion(bf16[2048,1024]{1,0:T(8,128)(2,1)} %param.3, bf16[2048,1024]{1,0:T(8,128)(2,1)} %all-gather.10.cloned.1.call-done), kind=kOutput, calls=%fused_computation.42 | convolution fusion | flops 4294967296 | bytes 12582912 | tf_op jit(solution)/shard_map/dot_general | solution.py:17
  67.1 0.8 slice.22
  67.9 2.3 slice.23
  70.3 101.9 %all-reduce.3.cloned.1.call-done = (f32[128,1024]{1,0:T(8,128)}, f32[896,1024]{1,0:T(8,128)}) async-done(((f32[128,1024]{1,0:T(8,128)}, f32[896,1024]{1,0:T(8,128)}), (f32[128,1024]{1,0:T(8,128)}, f32[896,1024]{1,0:T(8,128)})) %all-reduce.3.cloned.1.call-update) | async-done | bytes 4194320 | tf_op jit(solution)/shard_map/psum | solution.py:23
  172.2 1.9 broadcast_multiply_fusion.1
  174.2 46.9 %all-gather.12.cloned.1.call-done = f32[1024,1024]{1,0:T(8,128)} async-done(((f32[128,1024]{1,0:T(8,128)}), f32[1024,1024]{1,0:T(8,128)}) %all-gather.12.cloned.1.call-update) | async-done | bytes 4194320 | tf_op jit(solution)/shard_map/all_gather | solution.py:24
  221.2 17.1 %gather_fusion = f32[1024]{0:T(1024)S(1)} fusion(f32[1024,1024]{1,0:T(8,128)} %all-gather.12.cloned.1.call-done, s32[1024]{0:T(1024)S(1)} %bitcast.16), kind=kCustom, calls=%fused_computation | custom fusion | bytes 16384 | tf_op jit(solution)/shard_map/jit(diagonal)/cond/branch_0_fun/gather | solution.py:26
  238.2 0.6 reduce_sum.18
  239.5 3.9 multiply_reduce_fusion
  244.0 4.7 fusion.16
  248.8 2.5 fusion.28
  251.3 0.0 all-gather.16.cloned.1.call-start
  251.3 4.7 fusion.15
  256.0 23.4 %all-gather.14.cloned.1.call-done = bf16[1024,1024]{1,0:T(8,128)(2,1)} async-done(((bf16[128,1024]{1,0:T(8,128)(2,1)}), bf16[1024,1024]{1,0:T(8,128)(2,1)}) %all-gather.14.cloned.1.call-update) | async-done | bytes 2097168 | tf_op jit(solution)/shard_map/all_gather | solution.py:36
  279.4 3.3 fusion.29
  282.8 0.2 all-gather.18.cloned.1.call-start
  283.0 4.7 fusion.14
  287.7 23.8 %all-gather.16.cloned.1.call-done = bf16[1024,1024]{1,0:T(8,128)(2,1)} async-done(((bf16[128,1024]{1,0:T(8,128)(2,1)}), bf16[1024,1024]{1,0:T(8,128)(2,1)}) %all-gather.16.cloned.1.call-update) | async-done | bytes 2097168 | tf_op jit(solution)/shard_map/all_gather | solution.py:36
  311.5 3.3 fusion.30
  314.9 0.0 all-gather.8.cloned.1.call-start
  314.9 2.3 fusion.17
  317.2 0.0 all-gather.20.cloned.1.call-start
  317.3 4.7 fusion.13
  322.0 21.6 %all-gather.18.cloned.1.call-done = bf16[1024,1024]{1,0:T(8,128)(2,1)} async-done(((bf16[128,1024]{1,0:T(8,128)(2,1)}), bf16[1024,1024]{1,0:T(8,128)(2,1)}) %all-gather.18.cloned.1.call-update) | async-done | bytes 2097168 | tf_op jit(solution)/shard_map/all_gather | solution.py:36
  343.6 3.4 convolution_subtract_fusion
  347.0 4.6 broadcast_multiply_fusion
  351.6 40.8 %all-gather.8.cloned.1.call-done = bf16[2048,1024]{1,0:T(8,128)(2,1)} async-done(((bf16[2048,128]{1,0:T(8,128)(2,1)}), bf16[2048,1024]{1,0:T(8,128)(2,1)}) %all-gather.8.cloned.1.call-update) | async-done | bytes 4194320 | tf_op jit(solution)/shard_map/all_gather | solution.py:47
  392.4 46.7 %all-gather.20.cloned.1.call-done = f32[1024,1024]{1,0:T(8,128)} async-done(((f32[128,1024]{1,0:T(8,128)}), f32[1024,1024]{1,0:T(8,128)}) %all-gather.20.cloned.1.call-update) | async-done | bytes 4194320 | tf_op jit(solution)/shard_map/all_gather | solution.py:41
  439.1 16.8 %fusion.32 = f32[2048,1024]{1,0:T(8,128)S(1)} fusion(bf16[2048,1024]{1,0:T(8,128)(2,1)} %all-gather.8.cloned.1.call-done, f32[1024,1024]{1,0:T(8,128)} %all-gather.20.cloned.1.call-done), kind=kOutput, calls=%fused_computation.43 | convolution fusion | flops 25769803776 | bytes 16777216 | tf_op jit(solution)/shard_map/dot_general | solution.py:48
  455.9 30.5 %multiply_convert_fusion = bf16[2048,1024]{1,0:T(8,128)(2,1)} fusion(bf16[2048,1024]{1,0:T(8,128)(2,1)S(1)} %copy-done.2, s32[2048,1024]{1,0:T(8,128)} %param.5, f32[2048,1024]{1,0:T(8,128)S(1)} %fusion.32, f32[896,1024]{1,0:T(8,128)S(1)} %copy-done, f32[128,1024]{1,0:T(8,128)S(1)} %copy-done.1), kind=kOutput, calls=%fused_computation.1 | convolution fusion | flops 25781338112 | bytes 29360128 | tf_op jit(solution)/shard_map/dot_general | solution.py:49
  (20 shorter events, 0.3 us)
Async XLA Ops:
  6.5 53.0 %all-gather.10.cloned.1.call-start = ((), (), s32[]{:S(2)}) async-start(), calls=%async_computation.1 | async-start | bytes 4718592 | tf_op jit(solution)/shard_map/all_gather | solution.py:19
  8.4 163.8 %all-reduce.3.cloned.1.call-start = ((), (), s32[]{:S(2)}) async-start(), calls=%async_computation.7 | async-start | bytes 8388608 | tf_op jit(solution)/shard_map/psum | solution.py:23
  70.2 150.9 %all-gather.12.cloned.1.call-start = ((), (), s32[]{:S(2)}) async-start(), calls=%async_computation.2 | async-start | bytes 4718592 | tf_op jit(solution)/shard_map/all_gather | solution.py:24
  174.1 105.3 %all-gather.14.cloned.1.call-start = ((), (), s32[]{:S(2)}) async-start(), calls=%async_computation.3 | async-start | bytes 2359296 | tf_op jit(solution)/shard_map/all_gather | solution.py:36
  251.3 60.2 %all-gather.16.cloned.1.call-start = ((), (), s32[]{:S(2)}) async-start(), calls=%async_computation.4 | async-start | bytes 2359296 | tf_op jit(solution)/shard_map/all_gather | solution.py:36
  282.8 60.8 %all-gather.18.cloned.1.call-start = ((), (), s32[]{:S(2)}) async-start(), calls=%async_computation.5 | async-start | bytes 2359296 | tf_op jit(solution)/shard_map/all_gather | solution.py:36
  314.9 77.5 %all-gather.8.cloned.1.call-start = ((), (), s32[]{:S(2)}) async-start(), calls=%async_computation | async-start | bytes 4718592 | tf_op jit(solution)/shard_map/all_gather | solution.py:47
  317.2 121.8 %all-gather.20.cloned.1.call-start = ((), (), s32[]{:S(2)}) async-start(), calls=%async_computation.6 | async-start | bytes 4718592 | tf_op jit(solution)/shard_map/all_gather | solution.py:41
  351.6 104.3 %copy-start.1 = (f32[128,1024]{1,0:T(8,128)S(1)}, f32[128,1024]{1,0:T(8,128)}, u32[]{:S(2)}) copy-start(f32[128,1024]{1,0:T(8,128)} %broadcast_multiply_fusion.1) | copy-start | bytes 1572868
  439.1 16.8 %copy-start = (f32[896,1024]{1,0:T(8,128)S(1)}, f32[896,1024]{1,0:T(8,128)}, u32[]{:S(2)}) copy-start(f32[896,1024]{1,0:T(8,128)} %broadcast_multiply_fusion) | copy-start | bytes 11010052
  439.1 16.8 %copy-start.2 = (bf16[2048,1024]{1,0:T(8,128)(2,1)S(1)}, bf16[2048,1024]{1,0:T(8,128)(2,1)}, u32[]{:S(2)}) copy-start(bf16[2048,1024]{1,0:T(8,128)(2,1)} %param.4) | copy-start | bytes 12582916
Sparse Core Ops, SparseCore 0:
  8.9 50.5 all-gather.9
  70.3 101.8 all-reduce.2
  174.3 46.8 all-gather.11
  251.4 27.9 all-gather.13
  282.9 28.6 all-gather.15
  315.0 28.5 all-gather.17
  345.2 47.2 all-gather.7
  394.0 45.0 all-gather.19
where the time goes:
time: 494 us; the launch traced here: 493 us
  waiting for transfers between devices  356 us (72%)
  matrix products  86.3 us (17%)
  local copies, waits for them, and re-layouts  22.1 us (4%)
  between operations  14.9 us (3%)
  other arithmetic  13.3 us (3%)
    psum x1, waiting for transfers between devices, per_device(): block_part = lax.psum(partial_panel[:panel_width], 'tok') / total_count  102 us
    all_gather x3, waiting for transfers between devices, per_device(): lax.all_gather(iterate.astype(jnp.bfloat16), 'col', axis=0, tiled=True)  68.8 us
    all_gather x1, waiting for transfers between devices, per_device(): lax.all_gather(activations[:, :panel_width], 'col', axis=1, tiled=True)  51 us
    all_gather x1, waiting for transfers between devices, per_device(): diagonal_block = lax.all_gather(block_part, 'col', axis=0, tiled=True)  46.9 us
    all_gather x1, waiting for transfers between devices, per_device(): inverse = lax.all_gather(iterate, 'col', axis=0, tiled=True)  46.7 us
    all_gather x1, waiting for transfers between devices, per_device(): lax.all_gather(pruned, 'col', axis=1, tiled=True).astype(jnp.float32)  40.8 us
    dot_general x1, matrix products, per_device(): lax.dot_general(factor_rows, hessian_panel, (((1,), (1,)), ((), ())), pre...  30.5 us
    dot_general x4, matrix products, per_device(): product = jnp.dot(iterate, damped, precision=highest)  18.8 us
  transfers between devices with their start and end apart: 8, of which 8 were waited for; matrix products, arithmetic and copies ran while one was open for 5% of the time, Pallas kernels for 0%

commit v1 on v0

--- a/solution.py
+++ b/solution.py
@@ -16,7 +16,7 @@
     total_count = tok_rows * n_tok
     partial_panel = lax.dot_general(
         activations,
-        lax.all_gather(activations[:, :panel_width], "col", axis=1, tiled=True),
+        jnp.concatenate(lax.all_gather(activations[:, :panel_width], "col"), axis=1),
         (((0,), (0,)), ((), ())),
         preferred_element_type=jnp.float32,
     )

time: 494 us -> 501 us (1.014)
  local copies, waits for them, and re-layouts: 22.1 us -> 28.5 us
    reshape x0 -> x1, local copies, waits for them, and re-layouts: none -> 6.43 us  [per_device(): jnp.concatenate(lax.all_gather(activations[:, :panel_width], 'col'), axis=1)]
where the time goes in v1:
time: 501 us; the launch traced here: 499 us
  waiting for transfers between devices  356 us (71%)
  matrix products  86.4 us (17%)
  local copies, waits for them, and re-layouts  28.5 us (6%)
  between operations  14.9 us (3%)
  other arithmetic  13.3 us (3%)
    psum x1, waiting for transfers between devices, per_device(): block_part = lax.psum(partial_panel[:panel_width], 'tok') / total_count  103 us
    all_gather x3, waiting for transfers between devices, per_device(): lax.all_gather(iterate.astype(jnp.bfloat16), 'col', axis=0, tiled=True)  68.5 us
    all_gather x1, waiting for transfers between devices, per_device(): lax.all_gather(activations[:, :panel_width], 'col')  50.1 us
    all_gather x1, waiting for transfers between devices, per_device(): diagonal_block = lax.all_gather(block_part, 'col', axis=0, tiled=True)  46.9 us
    all_gather x1, waiting for transfers between devices, per_device(): inverse = lax.all_gather(iterate, 'col', axis=0, tiled=True)  46.7 us
    all_gather x1, waiting for transfers between devices, per_device(): lax.all_gather(pruned, 'col', axis=1, tiled=True).astype(jnp.float32)  40.8 us
    dot_general x1, matrix products, per_device(): lax.dot_general(factor_rows, hessian_panel, (((1,), (1,)), ((), ())), pre...  30.6 us
    dot_general x4, matrix products, per_device(): product = jnp.dot(iterate, damped, precision=highest)  18.8 us
  transfers between devices with their start and end apart: 8, of which 8 were waited for; matrix products, arithmetic and copies ran while one was open for 5% of the time, Pallas kernels for 0%

profile of v1, /device:TPU:0, one launch (start us, length us, event | category | flops | bytes accessed | tf_op | source)
XLA Modules:
  0.0 499.5 jit_solution(12740243283955924058)
XLA Ops:
  6.5 1.9 slice.17
  8.5 50.1 %all-gather.21.cloned.1.call-done = bf16[16384,128]{1,0:T(8,128)(2,1)} async-done(((bf16[2048,128]{1,0:T(8,128)(2,1)}), bf16[16384,128]{1,0:T(8,128)(2,1)}) %all-gather.21.cloned.1.call-update) | async-done | bytes 4194320 | tf_op jit(solution)/shard_map/all_gather | solution.py:19
  58.6 6.4 %copy.4 = bf16[2048,8,128]{0,2,1:T(8,128)(2,1)} copy(bf16[2048,8,128]{2,0,1:T(8,128)(2,1)} %bitcast.21) | data formatting | bytes 8388608 | tf_op jit(solution)/shard_map/reshape | solution.py:19
  65.0 7.6 %fusion.31 = f32[1024,1024]{1,0:T(8,128)S(1)} fusion(bf16[2048,1024]{1,0:T(8,128)(2,1)} %param.3, bf16[2048,1024]{0,1:T(8,128)(2,1)} %bitcast.22), kind=kOutput, calls=%fused_computation.42 | convolution fusion | flops 4294967296 | bytes 12582912 | tf_op jit(solution)/shard_map/dot_general | solution.py:17
  72.6 0.8 slice.22
  73.5 2.3 slice.23
  75.8 0.0 all-gather.11.cloned.1.call-start
  75.8 102.5 %all-reduce.3.cloned.1.call-done = (f32[128,1024]{1,0:T(8,128)}, f32[896,1024]{1,0:T(8,128)}) async-done(((f32[128,1024]{1,0:T(8,128)}, f32[896,1024]{1,0:T(8,128)}), (f32[128,1024]{1,0:T(8,128)}, f32[896,1024]{1,0:T(8,128)})) %all-reduce.3.cloned.1.call-update) | async-done | bytes 4194320 | tf_op jit(solution)/shard_map/psum | solution.py:23
  178.4 1.9 broadcast_multiply_fusion.1
  180.4 46.9 %all-gather.11.cloned.1.call-done = f32[1024,1024]{1,0:T(8,128)} async-done(((f32[128,1024]{1,0:T(8,128)}), f32[1024,1024]{1,0:T(8,128)}) %all-gather.11.cloned.1.call-update) | async-done | bytes 4194320 | tf_op jit(solution)/shard_map/all_gather | solution.py:24
  227.3 17.1 %gather_fusion = f32[1024]{0:T(1024)S(1)} fusion(f32[1024,1024]{1,0:T(8,128)} %all-gather.11.cloned.1.call-done, s32[1024]{0:T(1024)S(1)} %bitcast.20), kind=kCustom, calls=%fused_computation | custom fusion | bytes 16384 | tf_op jit(solution)/shard_map/jit(diagonal)/cond/branch_0_fun/gather | solution.py:26
  244.4 0.6 reduce_sum.18
  245.6 3.9 multiply_reduce_fusion
  250.2 4.7 fusion.16
  254.9 2.5 fusion.28
  257.5 0.2 all-gather.15.cloned.1.call-start
  257.7 4.7 fusion.15
  262.4 23.2 %all-gather.13.cloned.1.call-done = bf16[1024,1024]{1,0:T(8,128)(2,1)} async-done(((bf16[128,1024]{1,0:T(8,128)(2,1)}), bf16[1024,1024]{1,0:T(8,128)(2,1)}) %all-gather.13.cloned.1.call-update) | async-done | bytes 2097168 | tf_op jit(solution)/shard_map/all_gather | solution.py:36
  285.6 3.3 fusion.29
  289.0 4.7 fusion.14
  293.7 24.0 %all-gather.15.cloned.1.call-done = bf16[1024,1024]{1,0:T(8,128)(2,1)} async-done(((bf16[128,1024]{1,0:T(8,128)(2,1)}), bf16[1024,1024]{1,0:T(8,128)(2,1)}) %all-gather.15.cloned.1.call-update) | async-done | bytes 2097168 | tf_op jit(solution)/shard_map/all_gather | solution.py:36
  317.6 3.3 fusion.30
  321.0 2.3 fusion.17
  323.3 0.3 all-gather.19.cloned.1.call-start
  323.6 4.7 fusion.13
  328.3 21.4 %all-gather.17.cloned.1.call-done = bf16[1024,1024]{1,0:T(8,128)(2,1)} async-done(((bf16[128,1024]{1,0:T(8,128)(2,1)}), bf16[1024,1024]{1,0:T(8,128)(2,1)}) %all-gather.17.cloned.1.call-update) | async-done | bytes 2097168 | tf_op jit(solution)/shard_map/all_gather | solution.py:36
  349.7 3.4 convolution_subtract_fusion
  353.1 4.6 broadcast_multiply_fusion
  357.7 40.8 %all-gather.9.cloned.1.call-done = bf16[2048,1024]{1,0:T(8,128)(2,1)} async-done(((bf16[2048,128]{1,0:T(8,128)(2,1)}), bf16[2048,1024]{1,0:T(8,128)(2,1)}) %all-gather.9.cloned.1.call-update) | async-done | bytes 4194320 | tf_op jit(solution)/shard_map/all_gather | solution.py:47
  398.5 46.7 %all-gather.19.cloned.1.call-done = f32[1024,1024]{1,0:T(8,128)} async-done(((f32[128,1024]{1,0:T(8,128)}), f32[1024,1024]{1,0:T(8,128)}) %all-gather.19.cloned.1.call-update) | async-done | bytes 4194320 | tf_op jit(solution)/shard_map/all_gather | solution.py:41
  445.2 16.8 %fusion.32 = f32[2048,1024]{1,0:T(8,128)S(1)} fusion(bf16[2048,1024]{1,0:T(8,128)(2,1)} %all-gather.9.cloned.1.call-done, f32[1024,1024]{1,0:T(8,128)} %all-gather.19.cloned.1.call-done), kind=kOutput, calls=%fused_computation.43 | convolution fusion | flops 25769803776 | bytes 16777216 | tf_op jit(solution)/shard_map/dot_general | solution.py:48
  462.0 30.6 %multiply_convert_fusion = bf16[2048,1024]{1,0:T(8,128)(2,1)} fusion(bf16[2048,1024]{1,0:T(8,128)(2,1)S(1)} %copy-done.2, s32[2048,1024]{1,0:T(8,128)} %param.5, f32[2048,1024]{1,0:T(8,128)S(1)} %fusion.32, f32[896,1024]{1,0:T(8,128)S(1)} %copy-done, f32[128,1024]{1,0:T(8,128)S(1)} %copy-done.1), kind=kOutput, calls=%fused_computation.1 | convolution fusion | flops 25781338112 | bytes 29360128 | tf_op jit(solution)/shard_map/dot_general | solution.py:49
  (21 shorter events, 0.3 us)
Async XLA Ops:
  6.5 52.0 %all-gather.21.cloned.1.call-start = ((), (), s32[]{:S(2)}) async-start(), calls=%async_computation.6 | async-start | bytes 4718592 | tf_op jit(solution)/shard_map/all_gather | solution.py:19
  8.4 169.9 %all-reduce.3.cloned.1.call-start = ((), (), s32[]{:S(2)}) async-start(), calls=%async_computation.7 | async-start | bytes 8388608 | tf_op jit(solution)/shard_map/psum | solution.py:23
  75.8 151.5 %all-gather.11.cloned.1.call-start = ((), (), s32[]{:S(2)}) async-start(), calls=%async_computation.1 | async-start | bytes 4718592 | tf_op jit(solution)/shard_map/all_gather | solution.py:24
  180.3 105.3 %all-gather.13.cloned.1.call-start = ((), (), s32[]{:S(2)}) async-start(), calls=%async_computation.2 | async-start | bytes 2359296 | tf_op jit(solution)/shard_map/all_gather | solution.py:36
  257.5 60.2 %all-gather.15.cloned.1.call-start = ((), (), s32[]{:S(2)}) async-start(), calls=%async_computation.3 | async-start | bytes 2359296 | tf_op jit(solution)/shard_map/all_gather | solution.py:36
  288.9 60.8 %all-gather.17.cloned.1.call-start = ((), (), s32[]{:S(2)}) async-start(), calls=%async_computation.4 | async-start | bytes 2359296 | tf_op jit(solution)/shard_map/all_gather | solution.py:36
  321.0 77.5 %all-gather.9.cloned.1.call-start = ((), (), s32[]{:S(2)}) async-start(), calls=%async_computation | async-start | bytes 4718592 | tf_op jit(solution)/shard_map/all_gather | solution.py:47
  323.3 121.8 %all-gather.19.cloned.1.call-start = ((), (), s32[]{:S(2)}) async-start(), calls=%async_computation.5 | async-start | bytes 4718592 | tf_op jit(solution)/shard_map/all_gather | solution.py:41
  357.7 104.3 %copy-start.1 = (f32[128,1024]{1,0:T(8,128)S(1)}, f32[128,1024]{1,0:T(8,128)}, u32[]{:S(2)}) copy-start(f32[128,1024]{1,0:T(8,128)} %broadcast_multiply_fusion.1) | copy-start | bytes 1572868
  445.2 16.8 %copy-start = (f32[896,1024]{1,0:T(8,128)S(1)}, f32[896,1024]{1,0:T(8,128)}, u32[]{:S(2)}) copy-start(f32[896,1024]{1,0:T(8,128)} %broadcast_multiply_fusion) | copy-start | bytes 11010052
  445.2 16.8 %copy-start.2 = (bf16[2048,1024]{1,0:T(8,128)(2,1)S(1)}, bf16[2048,1024]{1,0:T(8,128)(2,1)}, u32[]{:S(2)}) copy-start(bf16[2048,1024]{1,0:T(8,128)(2,1)} %param.4) | copy-start | bytes 12582916
Sparse Core Ops, SparseCore 0:
  8.9 49.5 all-gather.20
  75.9 102.4 all-reduce.2
  180.4 46.8 all-gather.10
  257.6 27.9 all-gather.12
  289.1 28.5 all-gather.14
  321.1 28.5 all-gather.16
  351.3 47.1 all-gather.8
  400.1 45.0 all-gather.18
